TPU v7x, 32 devices: a whole 2x2x4 slice. The times are simulated.
32 devices in a mesh: groups: 1, ctx: 16 (over z, y, core), uly: 2 (over x), rep: 1.
Axes of the slice: x: 2, y: 2, z: 4, core: 2. Of those that a mesh axis runs over, the one named last changes fastest.
Arguments:
- q_proj: bfloat16 [4096, 5120], P(('groups', 'ctx', 'rep', 'uly')), may hold values from -8 to 8
- k_proj: bfloat16 [4096, 5120], P(('groups', 'ctx', 'rep', 'uly')), may hold values from -8 to 8
- v_proj: bfloat16 [4096, 5120], P(('groups', 'ctx', 'rep', 'uly')), may hold values from -4 to 4
- kv_list: int32 [32, 16], P('groups'), may hold values from -1 to 31, as said below
Outputs:
- attended: bfloat16 [4096, 5120], P(('groups', 'ctx', 'rep', 'uly'))
Inputs may be any that keep to these rules, and one draw needn't show every extreme that they name: `kv_list`: frame f holds blocks f * 2 to (f + 1) * 2 - 1. Row i lists, in ascending order and padded with -1 at the end, the key blocks that query block i attends: all 2 blocks of its own frame and some blocks of frames at distance 1 to 7. For a query frame f and a distance d whose frame f + d exists, the blocks of frame f + d listed by the query blocks of f are exactly 1 distinct blocks if |d| = 1 and exactly one block if 2 <= |d| <= 7; up to |d| = 3 every query block of f lists all of them.
All inputs are finite; a program needn't handle non-finite values.
Results may differ from a plain program's by a relative error of at most 0.014.
Values may be sent and summed in bfloat16 or wider, within the bound.
A program may use at most 128 MiB of HBM per device.

v0:
```python
import functools
import math

import jax
import jax.numpy as jnp
from jax import lax
from jax.experimental import pallas as pl
from jax.experimental.pallas import tpu as pltpu
from jax.sharding import PartitionSpec as P

HD = 128
BLK = 128
BPF = 2
FRAME = BLK * BPF
REACH = 7
GROUP = 8
SLOTS = 2 * REACH
KEYS = (SLOTS + BPF) * BLK

very_low = -1e30
scale2 = math.log2(math.e) / math.sqrt(HD)
MESH = pl.DeviceIdType.MESH


def kernel(sizes, sel_ref, bias_ref, q_ref, k_ref, v_ref, out_ref, kv, qb, ob, ks, vs,
           first_in, kv_in, q_in, kv_sent, q_sent, ring_in, ring_sent, out_in, out_sent):
    ctx, rep, uly, tokens, heads = sizes
    inner = GROUP // (rep * uly)
    here = GROUP * tokens
    frames_here = here // FRAME
    places = ctx // inner
    hops = -(-REACH // frames_here)
    c = lax.axis_index("ctx")
    r = lax.axis_index("rep")
    u = lax.axis_index("uly")
    place = c // inner
    me = (c % inner) * (rep * uly) + r * uly + u

    def member(j):
        return {"ctx": place * inner + j // (rep * uly), "rep": (j // uly) % rep, "uly": j % uly}

    def beside(step):
        return {"ctx": c + step * inner}

    has_left, has_right = place >= 1, place <= places - 2

    barrier = pltpu.get_barrier_semaphore()
    for k in range(1, GROUP):
        pl.semaphore_signal(barrier, inc=1, device_id=member((me + k) % GROUP), device_id_type=MESH)

    @pl.when(has_left)
    def _():
        pl.semaphore_signal(barrier, inc=1, device_id=beside(-1), device_id_type=MESH)

    @pl.when(has_right)
    def _():
        pl.semaphore_signal(barrier, inc=1, device_id=beside(1), device_id_type=MESH)

    neighbours = jnp.minimum(place, 1) + jnp.minimum(places - 1 - place, 1)
    pl.semaphore_wait(barrier, GROUP - 1 + neighbours)

    def columns(owner, h):
        return pl.ds(pl.multiple_of((owner * heads + h) * HD, HD), HD)

    own_rows = pl.ds(pl.multiple_of(REACH * FRAME + me * tokens, tokens), tokens)
    q_rows = pl.ds(pl.multiple_of(me * tokens, tokens), tokens)

    def share_kv(h, arrived):
        for k in range(1, GROUP):
            j = (me + k) % GROUP
            for which, src in enumerate((k_ref, v_ref)):
                pltpu.make_async_remote_copy(
                    src_ref=src.at[:, columns(j, h)], dst_ref=kv.at[h, which, own_rows],
                    send_sem=kv_sent.at[h], recv_sem=arrived(k),
                    device_id=member(j), device_id_type=MESH,
                ).start()
        for which, src in enumerate((k_ref, v_ref)):
            pltpu.make_async_copy(
                src.at[:, columns(me, h)], kv.at[h, which, own_rows], arrived(0)
            ).start()

    def share_later(h, carry):
        share_kv(h, lambda k: kv_in.at[h])
        return carry

    def share_q(h, carry):
        for k in range(1, GROUP):
            j = (me + k) % GROUP
            pltpu.make_async_remote_copy(
                src_ref=q_ref.at[:, columns(j, h)], dst_ref=qb.at[h, q_rows],
                send_sem=q_sent.at[h], recv_sem=q_in.at[h],
                device_id=member(j), device_id_type=MESH,
            ).start()
        pltpu.make_async_copy(q_ref.at[:, columns(me, h)], qb.at[h, q_rows], q_in.at[h]).start()
        return carry

    share_kv(0, lambda k: first_in.at[k])
    lax.fori_loop(1, heads, share_later, 0)
    lax.fori_loop(0, heads, share_q, 0)

    def await_bytes(ref, sem):
        pltpu.make_async_copy(ref, ref, sem).wait()

    def ring_copy(way, s, h):
        if way == 0:
            first, last, shift = max(0, REACH - s * frames_here), REACH - (s - 1) * frames_here, frames_here
        else:
            first = REACH + s * frames_here
            last, shift = min(frames_here + SLOTS, first + frames_here), -frames_here
        rows = (last - first) * FRAME
        return pltpu.make_async_remote_copy(
            src_ref=kv.at[h, :, pl.ds((first + shift) * FRAME, rows)],
            dst_ref=kv.at[h, :, pl.ds(first * FRAME, rows)],
            send_sem=ring_sent.at[way, s - 1, h], recv_sem=ring_in.at[way, s - 1, h],
            device_id=beside(1 if way == 0 else -1), device_id_type=MESH,
        )

    def sends(way, s):
        if way == 0:
            return (place >= s - 1) & has_right
        return (place + s <= places) & has_left

    def receives(way, s):
        return place >= s if way == 0 else place + s <= places - 1

    def ring_start(s, h):
        for way in (0, 1):
            @pl.when(sends(way, s))
            def _():
                ring_copy(way, s, h).start()

    def ring_arrived(s, h):
        for way in (0, 1):
            @pl.when(receives(way, s))
            def _():
                ring_copy(way, s, h).wait_recv()

    def attend(h):
        def one_frame(f, carry):
            own = pl.multiple_of((REACH + f) * FRAME, FRAME)
            ks[pl.ds(0, FRAME), :] = kv[h, 0, pl.ds(own, FRAME), :]
            vs[pl.ds(0, FRAME), :] = kv[h, 1, pl.ds(own, FRAME), :]

            def pick(i, carry):
                far = place * frames_here + f + i - REACH + i // REACH
                slot = jnp.minimum(jnp.maximum(far, 0), ctx - 1) - place * frames_here + REACH
                row = pl.multiple_of(slot * FRAME, FRAME)
                second = sel_ref[f, i] == 1
                to = pl.ds(pl.multiple_of(FRAME + i * BLK, BLK), BLK)
                for which, dst in ((0, ks), (1, vs)):
                    dst[to, :] = jnp.where(
                        second,
                        kv[h, which, pl.ds(row + BLK, BLK), :],
                        kv[h, which, pl.ds(row, BLK), :],
                    )
                return carry

            lax.fori_loop(0, SLOTS, pick, 0)

            def one_block(b, carry):
                rows = pl.ds(pl.multiple_of(f * FRAME + b * BLK, BLK), BLK)
                scores = lax.dot_general(
                    qb[h, rows, :], ks[...], (((1,), (1,)), ((), ())),
                    preferred_element_type=jnp.float32,
                )
                scores = scores * scale2 + bias_ref[f * BPF + b]
                weights = jnp.exp2(scores - jnp.max(scores, axis=1, keepdims=True))
                total = jnp.sum(weights, axis=1, keepdims=True)
                mixed = jnp.dot(
                    weights.astype(jnp.bfloat16), vs[...], preferred_element_type=jnp.float32
                )
                ob[h, rows, :] = (mixed / total).astype(jnp.bfloat16)
                return carry

            lax.fori_loop(0, BPF, one_block, 0)
            return carry

        lax.fori_loop(0, frames_here, one_frame, 0)

    def give_back(h):
        for k in range(1, GROUP):
            j = (me + k) % GROUP
            pltpu.make_async_remote_copy(
                src_ref=ob.at[h, pl.ds(pl.multiple_of(j * tokens, tokens), tokens)],
                dst_ref=out_ref.at[:, columns(me, h)],
                send_sem=out_sent.at[h], recv_sem=out_in.at[0],
                device_id=member(j), device_id_type=MESH,
            ).start()
        pltpu.make_async_copy(ob.at[h, q_rows], out_ref.at[:, columns(me, h)], out_in.at[0]).start()

    def step(t, carry):
        @pl.when((t >= 1) & (t < heads))
        def _():
            await_bytes(kv.at[t, :, pl.ds(REACH * FRAME, here)], kv_in.at[t])
            ring_start(1, t)

        for s in range(1, hops):
            @pl.when((t >= s) & (t < heads + s))
            def _():
                ring_arrived(s, t - s)
                ring_start(s + 1, t - s)

        @pl.when(t >= hops)
        def _():
            ring_arrived(hops, t - hops)
            await_bytes(qb.at[t - hops], q_in.at[t - hops])
            attend(t - hops)
            give_back(t - hops)

        return carry

    for k in range(GROUP):
        row = REACH * FRAME + (me + GROUP - k) % GROUP * tokens
        piece = kv.at[0, :, pl.ds(pl.multiple_of(row, tokens), tokens)]
        await_bytes(piece, first_in.at[k])
        for way in (0, 1):
            @pl.when(sends(way, 1))
            def _():
                to = row - here if way == 0 else row + here
                pltpu.make_async_remote_copy(
                    src_ref=piece, dst_ref=kv.at[0, :, pl.ds(pl.multiple_of(to, tokens), tokens)],
                    send_sem=ring_sent.at[way, 0, 0], recv_sem=ring_in.at[way, 0, 0],
                    device_id=beside(1 if way == 0 else -1), device_id_type=MESH,
                ).start()

    lax.fori_loop(0, heads + hops, step, 0)

    def finish(h, carry):
        others = (GROUP - 1) * tokens
        await_bytes(kv.at[h, :, pl.ds(0, others)], kv_sent.at[h])
        await_bytes(qb.at[h, pl.ds(0, others)], q_sent.at[h])
        await_bytes(ob.at[h, pl.ds(0, others)], out_sent.at[h])
        for s in range(1, hops + 1):
            for way in (0, 1):
                @pl.when(sends(way, s))
                def _():
                    ring_copy(way, s, h).wait_send()
        return carry

    lax.fori_loop(0, heads, finish, 0)
    await_bytes(out_ref, out_in.at[0])


def tables(kv_list, place, frames_here, frames):
    lists = lax.dynamic_slice_in_dim(kv_list, place * frames_here * BPF, frames_here * BPF, 0)
    lists = lists.reshape(frames_here, BPF, 1, -1)
    steps = jnp.array([d for d in range(-REACH, REACH + 1) if d != 0], jnp.int32)
    far = place * frames_here + jnp.arange(frames_here, dtype=jnp.int32)[:, None] + steps[None, :]
    inside = (far >= 0) & (far < frames)
    has = [jnp.any(lists == (far * BPF + b)[:, None, :, None], axis=3) for b in range(BPF)]
    listed = (has[0] | has[1]) & inside[:, None, :]
    sel = jnp.any(has[1], axis=1).astype(jnp.int32)
    bias = jnp.where(listed, 0.0, very_low).astype(jnp.float32)
    bias = jnp.concatenate([jnp.zeros((frames_here, BPF, BPF), jnp.float32), bias], axis=2)
    bias = jnp.repeat(bias.reshape(frames_here * BPF, BPF + SLOTS), BLK, axis=1)
    return sel, bias.reshape(frames_here * BPF, 1, KEYS)


def on_device(q_proj, k_proj, v_proj, kv_list):
    ctx, rep, uly = lax.axis_size("ctx"), lax.axis_size("rep"), lax.axis_size("uly")
    tokens, width = q_proj.shape
    heads = width // HD // GROUP
    inner = GROUP // (rep * uly)
    here = GROUP * tokens
    frames_here = here // FRAME
    hops = -(-REACH // frames_here)
    sel, bias = tables(kv_list, lax.axis_index("ctx") // inner, frames_here, ctx)
    window = (frames_here + SLOTS) * FRAME
    any_space = pl.BlockSpec(memory_space=pl.ANY)
    dma = pltpu.SemaphoreType.DMA
    return pl.pallas_call(
        functools.partial(kernel, (ctx, rep, uly, tokens, heads)),
        out_shape=jax.ShapeDtypeStruct((tokens, width), jnp.bfloat16),
        in_specs=[
            pl.BlockSpec(memory_space=pltpu.SMEM),
            pl.BlockSpec(memory_space=pltpu.VMEM),
            any_space, any_space, any_space,
        ],
        out_specs=any_space,
        scratch_shapes=[
            pltpu.VMEM((heads, 2, window, HD), jnp.bfloat16),
            pltpu.VMEM((heads, here, HD), jnp.bfloat16),
            pltpu.VMEM((heads, here, HD), jnp.bfloat16),
            pltpu.VMEM((KEYS, HD), jnp.bfloat16),
            pltpu.VMEM((KEYS, HD), jnp.bfloat16),
            dma((GROUP,)), dma((heads,)), dma((heads,)), dma((heads,)), dma((heads,)),
            dma((2, hops, heads)), dma((2, hops, heads)), dma((1,)), dma((heads,)),
        ],
        compiler_params=pltpu.CompilerParams(
            collective_id=0, has_side_effects=True, vmem_limit_bytes=56 * 1024 * 1024
        ),
    )(sel, bias, q_proj, k_proj, v_proj)


def solution(mesh):
    rows = P(("groups", "ctx", "rep", "uly"), None)
    return jax.shard_map(
        on_device,
        mesh=mesh,
        in_specs=(rows, rows, rows, P("groups", None)),
        out_specs=rows,
        check_vma=False,
    )
```

profile of v0, /device:TPU:0, one launch (start us, length us, event | category | flops | bytes accessed | tf_op | source)
XLA Modules:
  0.0 128.3 jit_solution(2351647441212999627)
XLA Ops:
  0.0 0.0 copy-start
  0.0 0.7 fusion
  0.7 0.0 copy-done
  0.7 0.1 constant_dynamic-slice_fusion
  0.8 0.1 copy.11
  0.9 0.7 add_multiply_fusion
  1.6 1.3 %compare_reduce_fusion = (pred[4,2,14]{0,2,1:T(8,128)(4,1)S(1)}, pred[4,14]{0,1:T(8,128)(4,1)S(1)}, pred[4,2,14]{0,2,1:T(8,128)(4,1)S(1)}) fusion(s32[4,14]{0,1:T(8,128)S(1)} %get-tuple-element.9, s32[4,2,16]{2,0,1:T(4,128)S(1)} %copy.8, s32[4,14]{0,1:T(8,128)S(1)} %get-tuple-element.8), kind=kLoop, calls=%fused_computation | loop fusion | flops 8680 | bytes 1240 | tf_op jit(solution)/shard_map/reduce_or | solution.py:250
  3.0 0.1 copy.9
  3.1 0.6 convert_element_type.3.sel_ref
  3.7 0.1 copy.12
  3.8 0.1 concatenate.3.clone
  3.9 0.7 broadcast_in_dim.18
  4.6 121.3 %shard_map.55 = bf16[128,5120]{1,0:T(8,128)(2,1)} custom-call(s32[4,14]{1,0:T(4,128)} %convert_element_type.3.sel_ref, f32[8,1,2048]{2,1,0:T(1,128)} %bitcast.3, bf16[128,5120]{1,0:T(8,128)(2,1)} %q_ref.1, bf16[128,5120]{1,0:T(8,128)(2,1)} %k_ref.1, bf16[128,5120]{1,0:T(8,128)(2,1)} %v_ref.1), custom_call_target="tpu_custom_call" | custom-call | tf_op jit(solution)/shard_map/pallas_call | solution.py:271
  125.9 2.5 %copy.14 = bf16[128,5120]{1,0:T(8,128)(2,1)} copy(bf16[128,5120]{1,0:T(8,128)(2,1)} %shard_map.55) | data formatting | bytes 2621440
  (3 shorter events, 0.0 us)
Async XLA Ops:
  0.0 0.7 copy-start
where the time goes:
time: 129 us; the launch traced here: 128 us
  Pallas kernels  121 us (94%)
  local copies, waits for them, and re-layouts  3.61 us (3%)
  other arithmetic  3.41 us (3%)
    pallas_call x1, Pallas kernels, on_device(): pl.pallas_call(functools.partial(kernel, (ctx, rep, uly, tokens, heads)),...  121 us
    unnamed x5, local copies, waits for them, and re-layouts  2.63 us

commit v1 on v0

--- a/solution.py
+++ b/solution.py
@@ -22,7 +22,7 @@
 MESH = pl.DeviceIdType.MESH
 
 
-def kernel(sizes, sel_ref, bias_ref, q_ref, k_ref, v_ref, out_ref, kv, qb, ob, ks, vs,
+def ring_kernel(sizes, sel_ref, bias_ref, q_ref, k_ref, v_ref, out_ref, kv, qb, ob, ks, vs,
            first_in, kv_in, q_in, kv_sent, q_sent, ring_in, ring_sent, out_in, out_sent):
     ctx, rep, uly, tokens, heads = sizes
     inner = GROUP // (rep * uly)
@@ -256,7 +256,7 @@
     return sel, bias.reshape(frames_here * BPF, 1, KEYS)
 
 
-def on_device(q_proj, k_proj, v_proj, kv_list):
+def ring_attention(q_proj, k_proj, v_proj, kv_list):
     ctx, rep, uly = lax.axis_size("ctx"), lax.axis_size("rep"), lax.axis_size("uly")
     tokens, width = q_proj.shape
     heads = width // HD // GROUP
@@ -269,7 +269,7 @@
     any_space = pl.BlockSpec(memory_space=pl.ANY)
     dma = pltpu.SemaphoreType.DMA
     return pl.pallas_call(
-        functools.partial(kernel, (ctx, rep, uly, tokens, heads)),
+        functools.partial(ring_kernel, (ctx, rep, uly, tokens, heads)),
         out_shape=jax.ShapeDtypeStruct((tokens, width), jnp.bfloat16),
         in_specs=[
             pl.BlockSpec(memory_space=pltpu.SMEM),
@@ -292,6 +292,414 @@
     )(sel, bias, q_proj, k_proj, v_proj)
 
 
+PLANE = 4
+NEAR = 3 * PLANE * FRAME
+NEAR_KEYS = NEAR // 2 + BLK
+FAR_SLOTS = 3
+FAR = (2 * FAR_SLOTS - 1) * BLK
+FAR_KEYS = FAR_SLOTS * BLK
+STEPS = 2 * REACH + 1
+PEERS = (2, 1, 3, 4, 6, 5, 7)
+
+
+def plane_kernel(ctx, heads, list_ref, q_ref, k_ref, v_ref, out_ref,
+                 lists, sel, listed, bias_near, bias_far, near, far, chosen, qb, ob, part, high, low, ks, vs,
+                 list_in, beside_in, plane_in, q_in, ring_in, far_in, out_in,
+                 plane_sent, q_sent, ring_sent, far_sent, out_sent):
+    here = PLANE * FRAME
+    places = ctx // PLANE
+    c = lax.axis_index("ctx")
+    u = lax.axis_index("uly")
+    place = c // PLANE
+    me = (c % PLANE) * BPF + u
+
+    def member(j):
+        return {"ctx": place * PLANE + j // BPF, "uly": j % BPF}
+
+    def beside(way):
+        return {"ctx": c + (PLANE if way == 0 else -PLANE)}
+
+    def peer(k):
+        bits = (me % 2, (me // 2) % 2, me // 4)
+        return sum((1 - bit if (k >> n) & 1 else bit) << n for n, bit in enumerate(bits))
+
+    has = (place <= places - 2, place >= 1)
+    gets = (place >= 1, place <= places - 2)
+    sends_far = ((place >= 1) & (place <= places - 2),) * 2
+    gets_far = (place >= 2, place <= places - 3)
+
+    barrier = pltpu.get_barrier_semaphore()
+    for way in (0, 1):
+        @pl.when(has[way])
+        def _():
+            pl.semaphore_signal(barrier, inc=1, device_id=beside(way), device_id_type=MESH)
+    for k in PEERS:
+        pl.semaphore_signal(barrier, inc=1, device_id=member(peer(k)), device_id_type=MESH)
+    neighbours = jnp.minimum(place, 1) + jnp.minimum(places - 1 - place, 1)
+    pl.semaphore_wait(barrier, GROUP - 1 + neighbours)
+
+    def columns(owner, h):
+        return pl.ds(pl.multiple_of((owner * heads + h) * HD, HD), HD)
+
+    def rows_of(j, base=0):
+        return pl.ds(pl.multiple_of(base + j * BLK, BLK), BLK)
+
+    def await_bytes(ref, sem):
+        pltpu.make_async_copy(ref, ref, sem).wait()
+
+    lands = (0, 2 * here)
+
+    def ring_own(h, carry):
+        for way in (0, 1):
+            @pl.when(has[way])
+            def _():
+                for which, src in enumerate((k_ref, v_ref)):
+                    pltpu.make_async_remote_copy(
+                        src_ref=src.at[:, columns(me, h)], dst_ref=near.at[h, which, rows_of(me, lands[way])],
+                        send_sem=ring_sent.at[way, h], recv_sem=ring_in.at[way, h],
+                        device_id=beside(way), device_id_type=MESH,
+                    ).start()
+        return carry
+
+    def ring_piece(h, j):
+        for way in (0, 1):
+            @pl.when(has[way])
+            def _():
+                pltpu.make_async_remote_copy(
+                    src_ref=near.at[h, :, rows_of(j, here)], dst_ref=near.at[h, :, rows_of(j, lands[way])],
+                    send_sem=ring_sent.at[way, h], recv_sem=ring_in.at[way, h],
+                    device_id=beside(way), device_id_type=MESH,
+                ).start()
+
+    def share_kv(h, carry):
+        for k in PEERS:
+            j = peer(k)
+            for which, src in enumerate((k_ref, v_ref)):
+                pltpu.make_async_remote_copy(
+                    src_ref=src.at[:, columns(j, h)], dst_ref=near.at[h, which, rows_of(me, here)],
+                    send_sem=plane_sent.at[h], recv_sem=(beside_in if k == 2 else plane_in).at[h],
+                    device_id=member(j), device_id_type=MESH,
+                ).start()
+        for which, src in enumerate((k_ref, v_ref)):
+            pltpu.make_async_copy(
+                src.at[:, columns(me, h)], near.at[h, which, rows_of(me, here)], plane_in.at[h]
+            ).start()
+        return carry
+
+    def share_q(h, carry):
+        for k in PEERS:
+            j = peer(k)
+            pltpu.make_async_remote_copy(
+                src_ref=q_ref.at[:, columns(j, h)], dst_ref=qb.at[h, rows_of(me)],
+                send_sem=q_sent.at[h], recv_sem=q_in.at[h],
+                device_id=member(j), device_id_type=MESH,
+            ).start()
+        pltpu.make_async_copy(q_ref.at[:, columns(me, h)], qb.at[h, rows_of(me)], q_in.at[h]).start()
+        return carry
+
+    lax.fori_loop(0, heads, ring_own, 0)
+    lax.fori_loop(0, heads, share_kv, 0)
+    lax.fori_loop(0, heads, share_q, 0)
+    get_lists = pltpu.make_async_copy(list_ref, lists, list_in.at[0])
+    get_lists.start()
+
+    def ring_beside(h, carry):
+        await_bytes(near.at[h, :, pl.ds(here, BLK)], beside_in.at[h])
+        ring_piece(h, peer(2))
+        return carry
+
+    lax.fori_loop(0, heads, ring_beside, 0)
+
+    for way in (0, 1):
+        @pl.when(jnp.logical_not(gets[way]))
+        def _():
+            def clear(h, carry):
+                for which in (0, 1):
+                    near[h, which, pl.ds(lands[way], here), :] = jnp.zeros((here, HD), jnp.bfloat16)
+                return carry
+
+            lax.fori_loop(0, heads, clear, 0)
+
+        @pl.when(jnp.logical_not(gets_far[way]))
+        def _():
+            def clear(h, carry):
+                for which in (0, 1):
+                    far[h, way, which] = jnp.zeros((FAR, HD), jnp.bfloat16)
+                return carry
+
+            lax.fori_loop(0, heads, clear, 0)
+
+    get_lists.wait()
+
+    def count(row, block):
+        return sum((lists[j, row] == block).astype(jnp.int32) for j in range(lists.shape[0]))
+
+    def tables(n, carry):
+        a, d = n // STEPS, n % STEPS
+        target = place * PLANE + a + d - REACH
+        block = jnp.where(target < 0, -BLK, target * BPF)
+        second = 0
+        for b in range(BPF):
+            row = (place * PLANE + a) * BPF + b
+            one = count(row, block + 1)
+            listed[a * BPF + b, d] = jnp.minimum(count(row, block) + one, 1)
+            second = second + one
+        sel[a, d] = jnp.minimum(second, 1)
+        return carry
+
+    lax.fori_loop(0, PLANE * STEPS, tables, 0)
+
+    def fill(ref, r, slot, d):
+        value = jnp.where(listed[r, d] == 1, 0.0, very_low)
+        ref[r, :, pl.ds(pl.multiple_of(slot * BLK, BLK), BLK)] = jnp.full((1, BLK), value, jnp.float32)
+
+    def biases(r, carry):
+        a = r // BPF
+        bias_near[r, :, pl.ds(0, FRAME)] = jnp.zeros((1, FRAME), jnp.float32)
+
+        def one_near(i, carry):
+            w = i + (i + REACH - PLANE - a) // REACH
+            fill(bias_near, r, BPF + i, jnp.minimum(w + REACH - PLANE - a, STEPS - 1))
+            return carry
+
+        def one_far(i, carry):
+            right = (i + a) // FAR_SLOTS
+            fill(bias_far, r, i, i + right * (STEPS - FAR_SLOTS))
+            return carry
+
+        lax.fori_loop(0, 3 * PLANE - 1, one_near, 0)
+        lax.fori_loop(0, FAR_SLOTS, one_far, 0)
+        return carry
+
+    lax.fori_loop(0, PLANE * BPF, biases, 0)
+
+    def ring_rest(h, carry):
+        await_bytes(near.at[h, :, pl.ds(here, here - BLK)], plane_in.at[h])
+        for k in PEERS[1:]:
+            ring_piece(h, peer(k))
+        return carry
+
+    lax.fori_loop(0, heads, ring_rest, 0)
+
+    frames = ctx
+    onward = (
+        (jnp.minimum((place + 1) * PLANE, frames - 1), place * PLANE - PLANE + 1),
+        (jnp.maximum((place - 1) * PLANE + PLANE - 1, 0), place * PLANE + PLANE + 2),
+    )
+    takes_second = [
+        (count(f * BPF, g * BPF + 1) + count(f * BPF + 1, g * BPF + 1)) > 0 for f, g in onward
+    ]
+
+    def far_copy(way, n, h):
+        b = 3 - n if way == 0 else 2 * PLANE + n
+        whole = n < FAR_SLOTS - 1
+        rows = FRAME if whole else BLK
+        return pltpu.make_async_remote_copy(
+            src_ref=near.at[h, :, pl.ds(b * FRAME, rows)] if whole else chosen.at[h, way],
+            dst_ref=far.at[h, way, :, pl.ds(n * FRAME, rows)],
+            send_sem=far_sent.at[way, n, h], recv_sem=far_in.at[way, n, h],
+            device_id=beside(way), device_id_type=MESH,
+        )
+
+    def attend_near(h):
+        def one_frame(a, carry):
+            own = pl.multiple_of((PLANE + a) * FRAME, FRAME)
+            ks[pl.ds(0, FRAME), :] = near[h, 0, pl.ds(own, FRAME), :]
+            vs[pl.ds(0, FRAME), :] = near[h, 1, pl.ds(own, FRAME), :]
+
+            def pick(i, carry):
+                w = i + (i + REACH - PLANE - a) // REACH
+                row = pl.multiple_of(w * FRAME, FRAME)
+                second = sel[a, jnp.minimum(w + REACH - PLANE - a, STEPS - 1)] == 1
+                to = pl.ds(pl.multiple_of(FRAME + i * BLK, BLK), BLK)
+                for which, dst in ((0, ks), (1, vs)):
+                    dst[to, :] = jnp.where(
+                        second, near[h, which, pl.ds(row + BLK, BLK), :], near[h, which, pl.ds(row, BLK), :]
+                    )
+                return carry
+
+            lax.fori_loop(0, 3 * PLANE - 1, pick, 0)
+            rows = pl.ds(pl.multiple_of(a * FRAME, FRAME), FRAME)
+            scores = lax.dot_general(
+                qb[h, rows, :], ks[...], (((1,), (1,)), ((), ())), preferred_element_type=jnp.float32
+            ).reshape(BPF, BLK, NEAR_KEYS)
+            scores = scores * scale2 + bias_near[pl.ds(a * BPF, BPF)]
+            top = jnp.max(scores, axis=2, keepdims=True)
+            weights = jnp.exp2(scores - top)
+            total = jnp.sum(weights, axis=2, keepdims=True)
+            part[h, rows, :] = jnp.dot(
+                weights.reshape(FRAME, NEAR_KEYS).astype(jnp.bfloat16), vs[...],
+                preferred_element_type=jnp.float32,
+            )
+            high[h, rows, :] = jnp.broadcast_to(top, (BPF, BLK, HD)).reshape(FRAME, HD)
+            low[h, rows, :] = jnp.broadcast_to(total, (BPF, BLK, HD)).reshape(FRAME, HD)
+            return carry
+
+        lax.fori_loop(0, PLANE, one_frame, 0)
+
+    def attend_far(h, a):
+        def pick(i, carry):
+            right = (i + a) // FAR_SLOTS
+            pair = (1 - right) * (FAR_SLOTS - 1 - a - i) + right * (i + a - FAR_SLOTS)
+            whole = 1 - pair // (FAR_SLOTS - 1)
+            row = pl.multiple_of(pair * FRAME, FRAME)
+            row_b = pl.multiple_of(pair * FRAME + whole * BLK, BLK)
+            second = sel[a, i + right * (STEPS - FAR_SLOTS)] == 1
+            to = pl.ds(pl.multiple_of(i * BLK, BLK), BLK)
+            for which, dst in ((0, ks), (1, vs)):
+                dst[to, :] = jnp.where(
+                    second, far[h, right, which, pl.ds(row_b, BLK), :], far[h, right, which, pl.ds(row, BLK), :]
+                )
+            return carry
+
+        lax.fori_loop(0, FAR_SLOTS, pick, 0)
+        rows = pl.ds(pl.multiple_of(a * FRAME, FRAME), FRAME)
+        keys = pl.ds(0, FAR_KEYS)
+        scores = lax.dot_general(
+            qb[h, rows, :], ks[keys, :], (((1,), (1,)), ((), ())), preferred_element_type=jnp.float32
+        ).reshape(BPF, BLK, FAR_KEYS)
+        scores = (scores * scale2 + bias_far[pl.ds(a * BPF, BPF)]).reshape(FRAME, FAR_KEYS)
+        before = high[h, rows, :]
+        top = jnp.maximum(before, jnp.max(scores, axis=1, keepdims=True))
+        weights = jnp.exp2(scores - jnp.concatenate([top] * FAR_SLOTS, axis=1))
+        fade = jnp.exp2(before - top)
+        total = fade * low[h, rows, :] + jnp.sum(weights, axis=1, keepdims=True)
+        mixed = fade * part[h, rows, :] + jnp.dot(
+            weights.astype(jnp.bfloat16), vs[keys, :], preferred_element_type=jnp.float32
+        )
+        ob[h, rows, :] = (mixed / total).astype(jnp.bfloat16)
+
+    def give_back(h, a):
+        for b in range(BPF):
+            j = a * BPF + b
+
+            @pl.when(j != me)
+            def _():
+                pltpu.make_async_remote_copy(
+                    src_ref=ob.at[h, rows_of(j)], dst_ref=out_ref.at[:, columns(me, h)],
+                    send_sem=out_sent.at[h], recv_sem=out_in.at[0],
+                    device_id=member(j), device_id_type=MESH,
+                ).start()
+
+            @pl.when(j == me)
+            def _():
+                pltpu.make_async_copy(ob.at[h, rows_of(j)], out_ref.at[:, columns(me, h)], out_in.at[0]).start()
+
+    def first_phase(h, carry):
+        for way in (0, 1):
+            @pl.when(gets[way])
+            def _():
+                await_bytes(near.at[h, :, pl.ds(lands[way], here)], ring_in.at[way, h])
+
+        for way in (0, 1):
+            @pl.when(sends_far[way])
+            def _():
+                frame = 1 if way == 0 else 2 * PLANE + 2
+                for which in (0, 1):
+                    chosen[h, way, which] = jnp.where(
+                        takes_second[way],
+                        near[h, which, pl.ds(frame * FRAME + BLK, BLK), :],
+                        near[h, which, pl.ds(frame * FRAME, BLK), :],
+                    )
+                for n in range(FAR_SLOTS):
+                    far_copy(way, n, h).start()
+
+        await_bytes(qb.at[h], q_in.at[h])
+        attend_near(h)
+        return carry
+
+    lax.fori_loop(0, heads, first_phase, 0)
+
+    both = gets_far[0] & gets_far[1]
+    falling = jnp.where(gets_far[0], 1, 0)
+
+    def second_phase(h, carry):
+        for way in (0, 1):
+            @pl.when(both)
+            def _():
+                for n in range(FAR_SLOTS):
+                    far_copy(way, n, h).wait_recv()
+
+        for n in range(PLANE):
+            if n >= 1:
+                for way in (0, 1):
+                    @pl.when(gets_far[way] & jnp.logical_not(both))
+                    def _():
+                        far_copy(way, n - 1, h).wait_recv()
+            a = falling * (PLANE - 1 - n) + (1 - falling) * n
+            attend_far(h, a)
+            give_back(h, a)
+        return carry
+
+    lax.fori_loop(0, heads, second_phase, 0)
+
+    def finish(h, carry):
+        others = (GROUP - 1) * BLK
+        await_bytes(near.at[h, :, pl.ds(0, others)], plane_sent.at[h])
+        await_bytes(qb.at[h, pl.ds(0, others)], q_sent.at[h])
+        await_bytes(ob.at[h, pl.ds(0, others)], out_sent.at[h])
+        for way in (0, 1):
+            @pl.when(has[way])
+            def _():
+                await_bytes(near.at[h, :, pl.ds(0, here)], ring_sent.at[way, h])
+
+            @pl.when(sends_far[way])
+            def _():
+                for n in range(FAR_SLOTS):
+                    far_copy(way, n, h).wait_send()
+        return carry
+
+    lax.fori_loop(0, heads, finish, 0)
+    await_bytes(out_ref, out_in.at[0])
+
+
+def plane_attention(q_proj, k_proj, v_proj, kv_list):
+    ctx = lax.axis_size("ctx")
+    tokens, width = q_proj.shape
+    heads = width // HD // GROUP
+    here = PLANE * FRAME
+    lists = kv_list.T
+    any_space = pl.BlockSpec(memory_space=pl.ANY)
+    dma = pltpu.SemaphoreType.DMA
+    bf16, f32 = jnp.bfloat16, jnp.float32
+    return pl.pallas_call(
+        functools.partial(plane_kernel, ctx, heads),
+        out_shape=jax.ShapeDtypeStruct((tokens, width), bf16),
+        in_specs=[any_space] * 4,
+        out_specs=any_space,
+        scratch_shapes=[
+            pltpu.SMEM(lists.shape, jnp.int32),
+            pltpu.SMEM((PLANE, STEPS), jnp.int32),
+            pltpu.SMEM((PLANE * BPF, STEPS), jnp.int32),
+            pltpu.VMEM((PLANE * BPF, 1, NEAR_KEYS), f32),
+            pltpu.VMEM((PLANE * BPF, 1, FAR_KEYS), f32),
+            pltpu.VMEM((heads, 2, NEAR, HD), bf16),
+            pltpu.VMEM((heads, 2, 2, FAR, HD), bf16),
+            pltpu.VMEM((heads, 2, 2, BLK, HD), bf16),
+            pltpu.VMEM((heads, here, HD), bf16),
+            pltpu.VMEM((heads, here, HD), bf16),
+            pltpu.VMEM((heads, here, HD), f32),
+            pltpu.VMEM((heads, here, HD), f32),
+            pltpu.VMEM((heads, here, HD), f32),
+            pltpu.VMEM((NEAR_KEYS, HD), bf16),
+            pltpu.VMEM((NEAR_KEYS, HD), bf16),
+            dma((1,)), dma((heads,)), dma((heads,)), dma((heads,)), dma((2, heads)),
+            dma((2, FAR_SLOTS, heads)), dma((1,)),
+            dma((heads,)), dma((heads,)), dma((2, heads)), dma((2, FAR_SLOTS, heads)), dma((heads,)),
+        ],
+        compiler_params=pltpu.CompilerParams(
+            collective_id=0, has_side_effects=True, vmem_limit_bytes=56 * 1024 * 1024
+        ),
+    )(lists, q_proj, k_proj, v_proj)
+
+
+def on_device(q_proj, k_proj, v_proj, kv_list):
+    rep, uly = lax.axis_size("rep"), lax.axis_size("uly")
+    if rep == 1 and uly == BPF and q_proj.shape[0] == BLK and lax.axis_size("ctx") % PLANE == 0:
+        return plane_attention(q_proj, k_proj, v_proj, kv_list)
+    return ring_attention(q_proj, k_proj, v_proj, kv_list)
+
+
 def solution(mesh):
     rows = P(("groups", "ctx", "rep", "uly"), None)
     return jax.shard_map(

time: 129 us -> 104 us (0.81)
  Pallas kernels: 121 us -> 102 us
  other arithmetic: 3.41 us -> 0 us
    pallas_call x1, Pallas kernels: 121 us -> 102 us  [plane_attention(): pl.pallas_call(functools.partial(plane_kernel, ctx, heads), out_shape=jax...]
    reduce_or x1 -> x0, other arithmetic: 1.34 us -> none  [tables(): jnp.any(lists == (far * BPF + b)[:, None, :, None], axis=3)]
    unnamed x5 -> x1, local copies, waits for them, and re-layouts: 2.63 us -> 2.46 us
where the time goes in v1:
time: 104 us
  Pallas kernels  102 us (98%)
  local copies, waits for them, and re-layouts  2.46 us (2%)
    pallas_call x1, Pallas kernels, plane_attention(): pl.pallas_call(functools.partial(plane_kernel, ctx, heads), out_shape=jax...  102 us
    unnamed x1, local copies, waits for them, and re-layouts  2.46 us

profile of v1, /device:TPU:0, one launch (start us, length us, event | category | flops | bytes accessed | tf_op | source)
XLA Modules:
  0.0 104.1 jit_solution(13061148308026370855)
XLA Ops:
  0.0 101.7 %shard_map.46 = bf16[128,5120]{1,0:T(8,128)(2,1)} custom-call(s32[16,32]{1,0:T(8,128)} %bitcast.1, bf16[128,5120]{1,0:T(8,128)(2,1)} %q_ref.1, bf16[128,5120]{1,0:T(8,128)(2,1)} %k_ref.1, bf16[128,5120]{1,0:T(8,128)(2,1)} %v_ref.1), custom_call_target="tpu_custom_call" | custom-call | tf_op jit(solution)/shard_map/pallas_call | solution.py:665
  101.7 2.5 %copy.6 = bf16[128,5120]{1,0:T(8,128)(2,1)} copy(bf16[128,5120]{1,0:T(8,128)(2,1)} %shard_map.46) | data formatting | bytes 2621440

commit v2 on v1

--- a/solution.py
+++ b/solution.py
@@ -688,9 +688,9 @@
             dma((heads,)), dma((heads,)), dma((2, heads)), dma((2, FAR_SLOTS, heads)), dma((heads,)),
         ],
         compiler_params=pltpu.CompilerParams(
-            collective_id=0, has_side_effects=True, vmem_limit_bytes=56 * 1024 * 1024
+            collective_id=0, has_side_effects=True, vmem_limit_bytes=30 * 1024 * 1024
         ),
-    )(lists, q_proj, k_proj, v_proj)
+    )(*[pltpu.with_memory_space_constraint(x, pltpu.HBM) for x in (lists, q_proj, k_proj, v_proj)])
 
 
 def on_device(q_proj, k_proj, v_proj, kv_list):

time: 104 us -> 103 us (level)
  local copies, waits for them, and re-layouts: 2.46 us -> 1.06 us
    unnamed x1, local copies, waits for them, and re-layouts: 2.46 us -> 1.06 us
where the time goes in v2:
time: 103 us
  Pallas kernels  102 us (99%)
  local copies, waits for them, and re-layouts  1.06 us (1%)
    pallas_call x1, Pallas kernels, plane_attention(): pl.pallas_call(functools.partial(plane_kernel, ctx, heads), out_shape=jax...  102 us

profile of v2, /device:TPU:0, one launch (start us, length us, event | category | flops | bytes accessed | tf_op | source)
XLA Modules:
  0.0 102.7 jit_solution(9531911470212904338)
XLA Ops:
  0.0 101.7 %shard_map.46 = bf16[128,5120]{1,0:T(8,128)(2,1)S(1)} custom-call(s32[16,32]{1,0:T(8,128)} %bitcast.1, bf16[128,5120]{1,0:T(8,128)(2,1)} %q_ref.1, bf16[128,5120]{1,0:T(8,128)(2,1)} %k_ref.1, bf16[128,5120]{1,0:T(8,128)(2,1)} %v_ref.1), custom_call_target="tpu_custom_call" | custom-call | tf_op jit(solution)/shard_map/pallas_call | solution.py:665
  101.7 1.1 %copy.6 = bf16[128,5120]{1,0:T(8,128)(2,1)} copy(bf16[128,5120]{1,0:T(8,128)(2,1)S(1)} %shard_map.46) | data formatting | bytes 2621440

commit v3 on v2

--- a/solution.py
+++ b/solution.py
@@ -304,7 +304,7 @@
 
 def plane_kernel(ctx, heads, list_ref, q_ref, k_ref, v_ref, out_ref,
                  lists, sel, listed, bias_near, bias_far, near, far, chosen, qb, ob, part, high, low, ks, vs,
-                 list_in, beside_in, plane_in, q_in, ring_in, far_in, out_in,
+                 list_in, own_in, beside_in, plane_in, q_in, ring_in, far_in, out_in,
                  plane_sent, q_sent, ring_sent, far_sent, out_sent):
     here = PLANE * FRAME
     places = ctx // PLANE
@@ -328,6 +328,22 @@
     sends_far = ((place >= 1) & (place <= places - 2),) * 2
     gets_far = (place >= 2, place <= places - 3)
 
+    def columns(owner, h):
+        return pl.ds(pl.multiple_of((owner * heads + h) * HD, HD), HD)
+
+    def rows_of(j, base=0):
+        return pl.ds(pl.multiple_of(base + j * BLK, BLK), BLK)
+
+    def await_bytes(ref, sem):
+        pltpu.make_async_copy(ref, ref, sem).wait()
+
+    def fetch_own(h, carry):
+        for which, src in enumerate((k_ref, v_ref)):
+            pltpu.make_async_copy(
+                src.at[:, columns(me, h)], near.at[h, which, rows_of(me, here)], own_in.at[h]
+            ).start()
+        return carry
+
     barrier = pltpu.get_barrier_semaphore()
     for way in (0, 1):
         @pl.when(has[way])
@@ -335,31 +351,11 @@
             pl.semaphore_signal(barrier, inc=1, device_id=beside(way), device_id_type=MESH)
     for k in PEERS:
         pl.semaphore_signal(barrier, inc=1, device_id=member(peer(k)), device_id_type=MESH)
+    lax.fori_loop(0, heads, fetch_own, 0)
     neighbours = jnp.minimum(place, 1) + jnp.minimum(places - 1 - place, 1)
     pl.semaphore_wait(barrier, GROUP - 1 + neighbours)
 
-    def columns(owner, h):
-        return pl.ds(pl.multiple_of((owner * heads + h) * HD, HD), HD)
-
-    def rows_of(j, base=0):
-        return pl.ds(pl.multiple_of(base + j * BLK, BLK), BLK)
-
-    def await_bytes(ref, sem):
-        pltpu.make_async_copy(ref, ref, sem).wait()
-
     lands = (0, 2 * here)
-
-    def ring_own(h, carry):
-        for way in (0, 1):
-            @pl.when(has[way])
-            def _():
-                for which, src in enumerate((k_ref, v_ref)):
-                    pltpu.make_async_remote_copy(
-                        src_ref=src.at[:, columns(me, h)], dst_ref=near.at[h, which, rows_of(me, lands[way])],
-                        send_sem=ring_sent.at[way, h], recv_sem=ring_in.at[way, h],
-                        device_id=beside(way), device_id_type=MESH,
-                    ).start()
-        return carry
 
     def ring_piece(h, j):
         for way in (0, 1):
@@ -380,10 +376,6 @@
                     send_sem=plane_sent.at[h], recv_sem=(beside_in if k == 2 else plane_in).at[h],
                     device_id=member(j), device_id_type=MESH,
                 ).start()
-        for which, src in enumerate((k_ref, v_ref)):
-            pltpu.make_async_copy(
-                src.at[:, columns(me, h)], near.at[h, which, rows_of(me, here)], plane_in.at[h]
-            ).start()
         return carry
 
     def share_q(h, carry):
@@ -395,6 +387,11 @@
                 device_id=member(j), device_id_type=MESH,
             ).start()
         pltpu.make_async_copy(q_ref.at[:, columns(me, h)], qb.at[h, rows_of(me)], q_in.at[h]).start()
+        return carry
+
+    def ring_own(h, carry):
+        await_bytes(near.at[h, :, pl.ds(here, BLK)], own_in.at[h])
+        ring_piece(h, me)
         return carry
 
     lax.fori_loop(0, heads, ring_own, 0)
@@ -474,7 +471,7 @@
     lax.fori_loop(0, PLANE * BPF, biases, 0)
 
     def ring_rest(h, carry):
-        await_bytes(near.at[h, :, pl.ds(here, here - BLK)], plane_in.at[h])
+        await_bytes(near.at[h, :, pl.ds(here, here - BPF * BLK)], plane_in.at[h])
         for k in PEERS[1:]:
             ring_piece(h, peer(k))
         return carry
@@ -613,7 +610,31 @@
     both = gets_far[0] & gets_far[1]
     falling = jnp.where(gets_far[0], 1, 0)
 
+    others = (GROUP - 1) * BLK
+
+    def await_far_sent(h):
+        for way in (0, 1):
+            @pl.when(sends_far[way])
+            def _():
+                for n in range(FAR_SLOTS):
+                    far_copy(way, n, h).wait_send()
+
+    def await_out_sent(h):
+        await_bytes(ob.at[h, pl.ds(0, others)], out_sent.at[h])
+
     def second_phase(h, carry):
+        await_bytes(near.at[h, :, pl.ds(0, others)], plane_sent.at[h])
+        await_bytes(qb.at[h, pl.ds(0, others)], q_sent.at[h])
+        for way in (0, 1):
+            @pl.when(has[way])
+            def _():
+                await_bytes(near.at[h, :, pl.ds(0, here)], ring_sent.at[way, h])
+
+        @pl.when(h >= 1)
+        def _():
+            await_far_sent(h - 1)
+            await_out_sent(h - 1)
+
         for way in (0, 1):
             @pl.when(both)
             def _():
@@ -633,23 +654,8 @@
 
     lax.fori_loop(0, heads, second_phase, 0)
 
-    def finish(h, carry):
-        others = (GROUP - 1) * BLK
-        await_bytes(near.at[h, :, pl.ds(0, others)], plane_sent.at[h])
-        await_bytes(qb.at[h, pl.ds(0, others)], q_sent.at[h])
-        await_bytes(ob.at[h, pl.ds(0, others)], out_sent.at[h])
-        for way in (0, 1):
-            @pl.when(has[way])
-            def _():
-                await_bytes(near.at[h, :, pl.ds(0, here)], ring_sent.at[way, h])
-
-            @pl.when(sends_far[way])
-            def _():
-                for n in range(FAR_SLOTS):
-                    far_copy(way, n, h).wait_send()
-        return carry
-
-    lax.fori_loop(0, heads, finish, 0)
+    await_far_sent(heads - 1)
+    await_out_sent(heads - 1)
     await_bytes(out_ref, out_in.at[0])
 
 
@@ -683,7 +689,7 @@
             pltpu.VMEM((heads, here, HD), f32),
             pltpu.VMEM((NEAR_KEYS, HD), bf16),
             pltpu.VMEM((NEAR_KEYS, HD), bf16),
-            dma((1,)), dma((heads,)), dma((heads,)), dma((heads,)), dma((2, heads)),
+            dma((1,)), dma((heads,)), dma((heads,)), dma((heads,)), dma((heads,)), dma((2, heads)),
             dma((2, FAR_SLOTS, heads)), dma((1,)),
             dma((heads,)), dma((heads,)), dma((2, heads)), dma((2, FAR_SLOTS, heads)), dma((heads,)),
         ],

time: 103 us -> 103 us (level)
  no operation moved by 1% of the time
where the time goes in v3:
time: 103 us
  Pallas kernels  101 us (98%)
  local copies, waits for them, and re-layouts  1.06 us (1%)
    pallas_call x1, Pallas kernels, plane_attention(): pl.pallas_call(functools.partial(plane_kernel, ctx, heads), out_shape=jax...  101 us

profile of v3, /device:TPU:0, one launch (start us, length us, event | category | flops | bytes accessed | tf_op | source)
XLA Modules:
  0.0 102.5 jit_solution(7244197529837051177)
XLA Ops:
  0.0 101.5 %shard_map.46 = bf16[128,5120]{1,0:T(8,128)(2,1)S(1)} custom-call(s32[16,32]{1,0:T(8,128)} %bitcast.1, bf16[128,5120]{1,0:T(8,128)(2,1)} %q_ref.1, bf16[128,5120]{1,0:T(8,128)(2,1)} %k_ref.1, bf16[128,5120]{1,0:T(8,128)(2,1)} %v_ref.1), custom_call_target="tpu_custom_call" | custom-call | tf_op jit(solution)/shard_map/pallas_call | solution.py:671
  101.5 1.1 %copy.6 = bf16[128,5120]{1,0:T(8,128)(2,1)} copy(bf16[128,5120]{1,0:T(8,128)(2,1)S(1)} %shard_map.46) | data formatting | bytes 2621440

commit v4 on v3

--- a/solution.py
+++ b/solution.py
@@ -566,9 +566,40 @@
         )
         ob[h, rows, :] = (mixed / total).astype(jnp.bfloat16)
 
+    def fold(h, a, n, last):
+        right = 1 - falling
+        i = falling * (FAR_SLOTS - 1 - a - n) + right * (n + FAR_SLOTS - a)
+        second = sel[a, i + right * (STEPS - FAR_SLOTS)] == 1
+        keys, values = [
+            far[h, right, which, pl.ds(n * FRAME, BLK), :] if n == FAR_SLOTS - 1 else jnp.where(
+                second, far[h, right, which, pl.ds(n * FRAME + BLK, BLK), :], far[h, right, which, pl.ds(n * FRAME, BLK), :]
+            )
+            for which in (0, 1)
+        ]
+        slot = pl.ds(pl.multiple_of(i * BLK, BLK), BLK)
+        rows = pl.ds(pl.multiple_of(a * FRAME, FRAME), FRAME)
+        scores = lax.dot_general(
+            qb[h, rows, :], keys, (((1,), (1,)), ((), ())), preferred_element_type=jnp.float32
+        ).reshape(BPF, BLK, BLK)
+        scores = (scores * scale2 + bias_far[pl.ds(a * BPF, BPF), :, slot]).reshape(FRAME, BLK)
+        before = high[h, rows, :]
+        top = jnp.maximum(before, jnp.max(scores, axis=1, keepdims=True))
+        weights = jnp.exp2(scores - top)
+        fade = jnp.exp2(before - top)
+        total = fade * low[h, rows, :] + jnp.sum(weights, axis=1, keepdims=True)
+        mixed = fade * part[h, rows, :] + jnp.dot(
+            weights.astype(jnp.bfloat16), values, preferred_element_type=jnp.float32
+        )
+        if last:
+            ob[h, rows, :] = (mixed / total).astype(jnp.bfloat16)
+        else:
+            high[h, rows, :] = top
+            low[h, rows, :] = total
+            part[h, rows, :] = mixed
+
     def give_back(h, a):
         for b in range(BPF):
-            j = a * BPF + b
+            j = a * BPF + (b + 1 - u) % BPF
 
             @pl.when(j != me)
             def _():
@@ -608,6 +639,7 @@
     lax.fori_loop(0, heads, first_phase, 0)
 
     both = gets_far[0] & gets_far[1]
+    neither = jnp.logical_not(gets_far[0] | gets_far[1])
     falling = jnp.where(gets_far[0], 1, 0)
 
     others = (GROUP - 1) * BLK
@@ -635,21 +667,39 @@
             await_far_sent(h - 1)
             await_out_sent(h - 1)
 
-        for way in (0, 1):
-            @pl.when(both)
-            def _():
-                for n in range(FAR_SLOTS):
-                    far_copy(way, n, h).wait_recv()
-
-        for n in range(PLANE):
-            if n >= 1:
+        @pl.when(both | neither)
+        def _():
+            for way in (0, 1):
+                @pl.when(both)
+                def _():
+                    for n in range(FAR_SLOTS):
+                        far_copy(way, n, h).wait_recv()
+
+            def one(a, carry):
+                attend_far(h, a)
+                give_back(h, a)
+                return carry
+
+            lax.fori_loop(0, PLANE, one, 0)
+
+        @pl.when(jnp.logical_not(both | neither))
+        def _():
+            free = falling * (PLANE - 1)
+            rows = pl.ds(pl.multiple_of(free * FRAME, FRAME), FRAME)
+            ob[h, rows, :] = (part[h, rows, :] / low[h, rows, :]).astype(jnp.bfloat16)
+            give_back(h, free)
+            for n in range(FAR_SLOTS):
                 for way in (0, 1):
-                    @pl.when(gets_far[way] & jnp.logical_not(both))
+                    @pl.when(gets_far[way])
                     def _():
-                        far_copy(way, n - 1, h).wait_recv()
-            a = falling * (PLANE - 1 - n) + (1 - falling) * n
-            attend_far(h, a)
-            give_back(h, a)
+                        far_copy(way, n, h).wait_recv()
+
+                done = falling * (FAR_SLOTS - 1 - n) + (1 - falling) * (n + 1)
+                fold(h, done, n, True)
+                give_back(h, done)
+                for j in range(1, FAR_SLOTS - n):
+                    fold(h, done + (1 - 2 * falling) * j, n, False)
+
         return carry
 
     lax.fori_loop(0, heads, second_phase, 0)

time: 103 us -> 103 us (level)
  no operation moved by 1% of the time
where the time goes in v4:
time: 103 us; the launch traced here: 102 us
  Pallas kernels  101 us (98%)
  local copies, waits for them, and re-layouts  1.06 us (1%)
    pallas_call x1, Pallas kernels, plane_attention(): pl.pallas_call(functools.partial(plane_kernel, ctx, heads), out_shape=jax...  101 us

profile of v4, /device:TPU:0, one launch (start us, length us, event | category | flops | bytes accessed | tf_op | source)
XLA Modules:
  0.0 102.4 jit_solution(258515978951091122)
XLA Ops:
  0.0 101.3 %shard_map.46 = bf16[128,5120]{1,0:T(8,128)(2,1)S(1)} custom-call(s32[16,32]{1,0:T(8,128)} %bitcast.1, bf16[128,5120]{1,0:T(8,128)(2,1)} %q_ref.1, bf16[128,5120]{1,0:T(8,128)(2,1)} %k_ref.1, bf16[128,5120]{1,0:T(8,128)(2,1)} %v_ref.1), custom_call_target="tpu_custom_call" | custom-call | tf_op jit(solution)/shard_map/pallas_call | solution.py:721
  101.3 1.1 %copy.6 = bf16[128,5120]{1,0:T(8,128)(2,1)} copy(bf16[128,5120]{1,0:T(8,128)(2,1)S(1)} %shard_map.46) | data formatting | bytes 2621440

commit v5 on v3

--- a/solution.py
+++ b/solution.py
@@ -550,37 +550,37 @@
             return carry
 
         lax.fori_loop(0, FAR_SLOTS, pick, 0)
-        rows = pl.ds(pl.multiple_of(a * FRAME, FRAME), FRAME)
         keys = pl.ds(0, FAR_KEYS)
-        scores = lax.dot_general(
-            qb[h, rows, :], ks[keys, :], (((1,), (1,)), ((), ())), preferred_element_type=jnp.float32
-        ).reshape(BPF, BLK, FAR_KEYS)
-        scores = (scores * scale2 + bias_far[pl.ds(a * BPF, BPF)]).reshape(FRAME, FAR_KEYS)
-        before = high[h, rows, :]
-        top = jnp.maximum(before, jnp.max(scores, axis=1, keepdims=True))
-        weights = jnp.exp2(scores - jnp.concatenate([top] * FAR_SLOTS, axis=1))
-        fade = jnp.exp2(before - top)
-        total = fade * low[h, rows, :] + jnp.sum(weights, axis=1, keepdims=True)
-        mixed = fade * part[h, rows, :] + jnp.dot(
-            weights.astype(jnp.bfloat16), vs[keys, :], preferred_element_type=jnp.float32
-        )
-        ob[h, rows, :] = (mixed / total).astype(jnp.bfloat16)
-
-    def give_back(h, a):
         for b in range(BPF):
-            j = a * BPF + b
-
-            @pl.when(j != me)
-            def _():
-                pltpu.make_async_remote_copy(
-                    src_ref=ob.at[h, rows_of(j)], dst_ref=out_ref.at[:, columns(me, h)],
-                    send_sem=out_sent.at[h], recv_sem=out_in.at[0],
-                    device_id=member(j), device_id_type=MESH,
-                ).start()
-
-            @pl.when(j == me)
-            def _():
-                pltpu.make_async_copy(ob.at[h, rows_of(j)], out_ref.at[:, columns(me, h)], out_in.at[0]).start()
+            j = a * BPF + (b + 1 - u) % BPF
+            rows = rows_of(j)
+            scores = lax.dot_general(
+                qb[h, rows, :], ks[keys, :], (((1,), (1,)), ((), ())), preferred_element_type=jnp.float32
+            )
+            scores = scores * scale2 + bias_far[j]
+            before = high[h, rows, :]
+            top = jnp.maximum(before, jnp.max(scores, axis=1, keepdims=True))
+            weights = jnp.exp2(scores - jnp.concatenate([top] * FAR_SLOTS, axis=1))
+            fade = jnp.exp2(before - top)
+            total = fade * low[h, rows, :] + jnp.sum(weights, axis=1, keepdims=True)
+            mixed = fade * part[h, rows, :] + jnp.dot(
+                weights.astype(jnp.bfloat16), vs[keys, :], preferred_element_type=jnp.float32
+            )
+            ob[h, rows, :] = (mixed / total).astype(jnp.bfloat16)
+            give_back(h, j)
+
+    def give_back(h, j):
+        @pl.when(j != me)
+        def _():
+            pltpu.make_async_remote_copy(
+                src_ref=ob.at[h, rows_of(j)], dst_ref=out_ref.at[:, columns(me, h)],
+                send_sem=out_sent.at[h], recv_sem=out_in.at[0],
+                device_id=member(j), device_id_type=MESH,
+            ).start()
+
+        @pl.when(j == me)
+        def _():
+            pltpu.make_async_copy(ob.at[h, rows_of(j)], out_ref.at[:, columns(me, h)], out_in.at[0]).start()
 
     def first_phase(h, carry):
         for way in (0, 1):
@@ -649,7 +649,6 @@
                         far_copy(way, n - 1, h).wait_recv()
             a = falling * (PLANE - 1 - n) + (1 - falling) * n
             attend_far(h, a)
-            give_back(h, a)
         return carry
 
     lax.fori_loop(0, heads, second_phase, 0)

time: 103 us -> 103 us (level)
  no operation moved by 1% of the time
where the time goes in v5:
time: 103 us; the launch traced here: 102 us
  Pallas kernels  101 us (98%)
  local copies, waits for them, and re-layouts  1.06 us (1%)
    pallas_call x1, Pallas kernels, plane_attention(): pl.pallas_call(functools.partial(plane_kernel, ctx, heads), out_shape=jax...  101 us

profile of v5, /device:TPU:0, one launch (start us, length us, event | category | flops | bytes accessed | tf_op | source)
XLA Modules:
  0.0 102.5 jit_solution(13863977981318525276)
XLA Ops:
  0.0 101.4 %shard_map.46 = bf16[128,5120]{1,0:T(8,128)(2,1)S(1)} custom-call(s32[16,32]{1,0:T(8,128)} %bitcast.1, bf16[128,5120]{1,0:T(8,128)(2,1)} %q_ref.1, bf16[128,5120]{1,0:T(8,128)(2,1)} %k_ref.1, bf16[128,5120]{1,0:T(8,128)(2,1)} %v_ref.1), custom_call_target="tpu_custom_call" | custom-call | tf_op jit(solution)/shard_map/pallas_call | solution.py:670
  101.4 1.1 %copy.6 = bf16[128,5120]{1,0:T(8,128)(2,1)} copy(bf16[128,5120]{1,0:T(8,128)(2,1)S(1)} %shard_map.46) | data formatting | bytes 2621440

commit v6 on v3

--- a/solution.py
+++ b/solution.py
@@ -358,7 +358,7 @@
     lands = (0, 2 * here)
 
     def ring_piece(h, j):
-        for way in (0, 1):
+        for way in (1, 0):
             @pl.when(has[way])
             def _():
                 pltpu.make_async_remote_copy(
@@ -588,7 +588,7 @@
             def _():
                 await_bytes(near.at[h, :, pl.ds(lands[way], here)], ring_in.at[way, h])
 
-        for way in (0, 1):
+        for way in (1, 0):
             @pl.when(sends_far[way])
             def _():
                 frame = 1 if way == 0 else 2 * PLANE + 2

time: 103 us -> 103 us (level)
  no operation moved by 1% of the time
where the time goes in v6:
time: 103 us
  Pallas kernels  101 us (98%)
  local copies, waits for them, and re-layouts  1.06 us (1%)
    pallas_call x1, Pallas kernels, plane_attention(): pl.pallas_call(functools.partial(plane_kernel, ctx, heads), out_shape=jax...  101 us

profile of v6, /device:TPU:0, one launch (start us, length us, event | category | flops | bytes accessed | tf_op | source)
XLA Modules:
  0.0 102.5 jit_solution(4614376402538920462)
XLA Ops:
  0.0 101.5 %shard_map.46 = bf16[128,5120]{1,0:T(8,128)(2,1)S(1)} custom-call(s32[16,32]{1,0:T(8,128)} %bitcast.1, bf16[128,5120]{1,0:T(8,128)(2,1)} %q_ref.1, bf16[128,5120]{1,0:T(8,128)(2,1)} %k_ref.1, bf16[128,5120]{1,0:T(8,128)(2,1)} %v_ref.1), custom_call_target="tpu_custom_call" | custom-call | tf_op jit(solution)/shard_map/pallas_call | solution.py:671
  101.5 1.1 %copy.6 = bf16[128,5120]{1,0:T(8,128)(2,1)} copy(bf16[128,5120]{1,0:T(8,128)(2,1)S(1)} %shard_map.46) | data formatting | bytes 2621440

commit v7 on v3

--- a/solution.py
+++ b/solution.py
@@ -305,7 +305,7 @@
 def plane_kernel(ctx, heads, list_ref, q_ref, k_ref, v_ref, out_ref,
                  lists, sel, listed, bias_near, bias_far, near, far, chosen, qb, ob, part, high, low, ks, vs,
                  list_in, own_in, beside_in, plane_in, q_in, ring_in, far_in, out_in,
-                 plane_sent, q_sent, ring_sent, far_sent, out_sent):
+                 plane_sent, q_sent, ring_sent, far_sent, out_sent, ready):
     here = PLANE * FRAME
     places = ctx // PLANE
     c = lax.axis_index("ctx")
@@ -345,20 +345,23 @@
         return carry
 
     barrier = pltpu.get_barrier_semaphore()
-    for way in (0, 1):
-        @pl.when(has[way])
-        def _():
-            pl.semaphore_signal(barrier, inc=1, device_id=beside(way), device_id_type=MESH)
+    @pl.when(has[0])
+    def _():
+        pl.semaphore_signal(barrier, inc=1, device_id=beside(0), device_id_type=MESH)
+
     for k in PEERS:
         pl.semaphore_signal(barrier, inc=1, device_id=member(peer(k)), device_id_type=MESH)
     lax.fori_loop(0, heads, fetch_own, 0)
-    neighbours = jnp.minimum(place, 1) + jnp.minimum(places - 1 - place, 1)
-    pl.semaphore_wait(barrier, GROUP - 1 + neighbours)
+    pl.semaphore_wait(barrier, GROUP - 1 + jnp.minimum(place, 1))
+
+    @pl.when(has[1])
+    def _():
+        pl.semaphore_signal(ready, inc=1, device_id=beside(1), device_id_type=MESH)
 
     lands = (0, 2 * here)
 
-    def ring_piece(h, j):
-        for way in (0, 1):
+    def ring_piece(h, j, ways=(0, 1)):
+        for way in ways:
             @pl.when(has[way])
             def _():
                 pltpu.make_async_remote_copy(
@@ -389,13 +392,23 @@
         pltpu.make_async_copy(q_ref.at[:, columns(me, h)], qb.at[h, rows_of(me)], q_in.at[h]).start()
         return carry
 
-    def ring_own(h, carry):
+    def own_left(h, carry):
         await_bytes(near.at[h, :, pl.ds(here, BLK)], own_in.at[h])
-        ring_piece(h, me)
-        return carry
-
-    lax.fori_loop(0, heads, ring_own, 0)
+        ring_piece(h, me, (1,))
+        return carry
+
+    def own_right(h, carry):
+        ring_piece(h, me, (0,))
+        return carry
+
+    lax.fori_loop(0, heads, own_left, 0)
     lax.fori_loop(0, heads, share_kv, 0)
+
+    @pl.when(has[0])
+    def _():
+        pl.semaphore_wait(ready, 1)
+
+    lax.fori_loop(0, heads, own_right, 0)
     lax.fori_loop(0, heads, share_q, 0)
     get_lists = pltpu.make_async_copy(list_ref, lists, list_in.at[0])
     get_lists.start()
@@ -692,6 +705,7 @@
             dma((1,)), dma((heads,)), dma((heads,)), dma((heads,)), dma((heads,)), dma((2, heads)),
             dma((2, FAR_SLOTS, heads)), dma((1,)),
             dma((heads,)), dma((heads,)), dma((2, heads)), dma((2, FAR_SLOTS, heads)), dma((heads,)),
+            pltpu.SemaphoreType.REGULAR,
         ],
         compiler_params=pltpu.CompilerParams(
             collective_id=0, has_side_effects=True, vmem_limit_bytes=30 * 1024 * 1024

time: 103 us -> 103 us (level)
  no operation moved by 1% of the time
where the time goes in v7:
time: 103 us
  Pallas kernels  102 us (99%)
  local copies, waits for them, and re-layouts  1.06 us (1%)
    pallas_call x1, Pallas kernels, plane_attention(): pl.pallas_call(functools.partial(plane_kernel, ctx, heads), out_shape=jax...  102 us

profile of v7, /device:TPU:0, one launch (start us, length us, event | category | flops | bytes accessed | tf_op | source)
XLA Modules:
  0.0 102.6 jit_solution(14727650124577722326)
XLA Ops:
  0.0 101.5 %shard_map.46 = bf16[128,5120]{1,0:T(8,128)(2,1)S(1)} custom-call(s32[16,32]{1,0:T(8,128)} %bitcast.1, bf16[128,5120]{1,0:T(8,128)(2,1)} %q_ref.1, bf16[128,5120]{1,0:T(8,128)(2,1)} %k_ref.1, bf16[128,5120]{1,0:T(8,128)(2,1)} %v_ref.1), custom_call_target="tpu_custom_call" | custom-call | tf_op jit(solution)/shard_map/pallas_call | solution.py:684
  101.5 1.1 %copy.6 = bf16[128,5120]{1,0:T(8,128)(2,1)} copy(bf16[128,5120]{1,0:T(8,128)(2,1)S(1)} %shard_map.46) | data formatting | bytes 2621440
